TPU v7x, 32 devices: a whole 2x2x4 slice. The times are simulated.
32 devices in a mesh: fsdp: 4 (over y, x), heads: 2 (over core), tensor: 4 (over z).
Axes of the slice: x: 2, y: 2, z: 4, core: 2. Of those that a mesh axis runs over, the one named last changes fastest.
Arguments:
- inputs: float32 [32, 729, 1152], P(('fsdp', 'heads', 'tensor')), may hold values from -6 to 6
- cotangent: float32 [32, 729, 1152], P(('fsdp', 'heads', 'tensor')), may hold values from -6 to 6
- image_adapter_index: int32 [32], replicated, may hold values from 0 to 7
- first_norm_gain: float32 [1152], replicated, may hold values from 0.5 to 1.5
- first_norm_bias: float32 [1152], replicated, may hold values from -3 to 3
- second_norm_gain: float32 [1152], replicated, may hold values from 0.5 to 1.5
- second_norm_bias: float32 [1152], replicated, may hold values from -3 to 3
- query_key_value_weight: bfloat16 [1152, 3, 1152], P('fsdp', None, 'heads'), may hold values from -0.1875 to 0.1875
- attention_output_weight: bfloat16 [1152, 1152], P('fsdp', 'heads'), may hold values from -3 to 3
- up_weight: bfloat16 [1152, 4304], P('fsdp', 'tensor'), may hold values from -0.1875 to 0.1875
- down_weight: bfloat16 [1152, 4304], P('fsdp', 'tensor'), may hold values from -0.09375 to 0.09375
- up_projection_bias: bfloat16 [4304], P('tensor'), may hold values from -3 to 3
- down_projection_bias: bfloat16 [1152], replicated, may hold values from -3 to 3
- query_key_value_adapter_first: bfloat16 [3, 8, 1152, 16], replicated, may hold values from -0.1875 to 0.1875
- query_key_value_adapter_second: bfloat16 [3, 8, 16, 1152], P(None, None, None, 'heads'), may hold values from -0.75 to 0.75
- projection_adapter_first: bfloat16 [8, 1152, 16], P(None, 'heads'), may hold values from -3 to 3
- projection_adapter_second: bfloat16 [8, 16, 1152], replicated, may hold values from -0.75 to 0.75
- up_adapter_first: bfloat16 [8, 1152, 16], replicated, may hold values from -0.1875 to 0.1875
- up_adapter_second: bfloat16 [8, 16, 4304], P(None, None, 'tensor'), may hold values from -0.75 to 0.75
- down_adapter_first: bfloat16 [8, 16, 4304], P(None, None, 'tensor'), may hold values from -0.09375 to 0.09375
- down_adapter_second: bfloat16 [8, 16, 1152], replicated, may hold values from -0.75 to 0.75
Outputs:
- layer_output: float32 [32, 729, 1152], P(('fsdp', 'heads', 'tensor'))
- grad_input: float32 [32, 729, 1152], P(('fsdp', 'heads', 'tensor'))
- grad_qkv_in: float32 [3, 8, 1152, 16], replicated
- grad_qkv_out: float32 [3, 8, 16, 1152], P(None, None, None, 'heads')
- grad_proj_in: float32 [8, 1152, 16], P(None, 'heads')
- grad_proj_out: float32 [8, 16, 1152], replicated
- grad_up_in: float32 [8, 1152, 16], replicated
- grad_up_out: float32 [8, 16, 4304], P(None, None, 'tensor')
- grad_down_in: float32 [8, 16, 4304], P(None, None, 'tensor')
- grad_down_out: float32 [8, 16, 1152], replicated
All inputs are finite; a program needn't handle non-finite values.
Results may differ from a plain program's by a relative error of at most 0.02.
Values may be sent and summed in bfloat16 or wider, within the bound.
A program may use at most 256 MiB of HBM per device.

v0:
```python
import jax
import jax.numpy as jnp
from jax import lax
from jax.sharding import PartitionSpec as P

HEAD_DIM = 72
highest_precision = lax.Precision.HIGHEST
norm_eps = 1e-06


def normalize(values, gain, bias):
    mean = jnp.mean(values, axis=-1, keepdims=True)
    centred = values - mean
    inverse = lax.rsqrt(jnp.mean(centred * centred, axis=-1, keepdims=True) + norm_eps)
    unit = centred * inverse
    return (unit * gain + bias, unit, inverse)


def normalize_back(grad_norm, unit, inverse, gain):
    scaled = grad_norm * gain
    return inverse * (
        scaled
        - jnp.mean(scaled, axis=-1, keepdims=True)
        - unit * jnp.mean(scaled * unit, axis=-1, keepdims=True)
    )


def gelu_tanh(values):
    return jax.nn.gelu(values, approximate=True)


def one_hot(ids, count):
    return (ids[:, None] == jnp.arange(count, dtype=jnp.int32)[None, :]).astype(jnp.float32)


def by_adapter(hot, per_image):
    return jnp.einsum("ia,ixy->axy", hot, per_image, precision=highest_precision)


def attend_forward(operands):
    query, keyed, valued = operands
    scores = jnp.einsum(
        "qhd,khd->hqk", query, keyed, preferred_element_type=jnp.float32
    ) * HEAD_DIM ** (-0.5)
    top = jnp.max(scores, axis=-1, keepdims=True)
    weights = jnp.exp(scores - top)
    total = jnp.sum(weights, axis=-1, keepdims=True)
    probs = (weights / total).astype(jnp.bfloat16)
    mixed_heads = jnp.einsum("hqk,khd->qhd", probs, valued, preferred_element_type=jnp.float32)
    return (mixed_heads.astype(jnp.bfloat16), (top + jnp.log(total))[..., 0])


def attend_back(operands):
    query, keyed, valued, grad_mixed, log_total = operands
    scale = HEAD_DIM ** (-0.5)
    scores = jnp.einsum("qhd,khd->hqk", query, keyed, preferred_element_type=jnp.float32) * scale
    probs = jnp.exp(scores - log_total[..., None])
    grad_probs = jnp.einsum("qhd,khd->hqk", grad_mixed, valued, preferred_element_type=jnp.float32)
    grad_values = jnp.einsum(
        "hqk,qhd->khd", probs.astype(jnp.bfloat16), grad_mixed, preferred_element_type=jnp.float32
    )
    inner = jnp.sum(probs * grad_probs, axis=-1, keepdims=True)
    grad_scores = (probs * (grad_probs - inner)).astype(jnp.bfloat16)
    grad_query = (
        jnp.einsum("hqk,khd->qhd", grad_scores, keyed, preferred_element_type=jnp.float32) * scale
    )
    grad_keys = (
        jnp.einsum("hqk,qhd->khd", grad_scores, query, preferred_element_type=jnp.float32) * scale
    )
    return (grad_query, grad_keys, grad_values)


def per_device(
    inputs,
    cotangent,
    image_adapter_index,
    first_norm_gain,
    first_norm_bias,
    second_norm_gain,
    second_norm_bias,
    query_key_value_weight,
    attention_output_weight,
    up_weight,
    down_weight,
    up_projection_bias,
    down_projection_bias,
    query_key_value_adapter_first,
    query_key_value_adapter_second,
    projection_adapter_first,
    projection_adapter_second,
    up_adapter_first,
    up_adapter_second,
    down_adapter_first,
    down_adapter_second,
):
    head_count = lax.axis_size("heads")
    unit_count = lax.axis_size("tensor")
    fsdp_index = lax.axis_index("fsdp")
    head_index = lax.axis_index("heads")
    unit_index = lax.axis_index("tensor")
    images, length, width = inputs.shape
    adapter_factors = query_key_value_adapter_first.shape[1]
    local = jnp.arange(images, dtype=jnp.int32)
    group = fsdp_index * head_count
    own_rows = ((group + head_index) * unit_count + unit_index) * images + local
    head_rows = (
        ((group + jnp.arange(head_count, dtype=jnp.int32))[:, None] * unit_count + unit_index)
        * images
        + local[None, :]
    ).reshape(-1)
    unit_rows = (
        ((group + head_index) * unit_count + jnp.arange(unit_count, dtype=jnp.int32))[:, None]
        * images
        + local[None, :]
    ).reshape(-1)
    owned_numbers = image_adapter_index[own_rows]
    head_numbers = image_adapter_index[head_rows]
    unit_numbers = image_adapter_index[unit_rows]
    query_key_value_whole, output_whole_weight, up_rows, down_rows = (
        lax.all_gather(query_key_value_weight, "fsdp", axis=0, tiled=True),
        lax.all_gather(attention_output_weight, "fsdp", axis=0, tiled=True),
        lax.all_gather(up_weight, "fsdp", axis=0, tiled=True),
        lax.all_gather(down_weight, "fsdp", axis=0, tiled=True),
    )
    norm1, unit1, inverse1 = normalize(inputs, first_norm_gain, first_norm_bias)
    ln1_all = lax.all_gather(norm1.astype(jnp.bfloat16), "heads", axis=0, tiled=True)
    (
        query_key_value_attention,
        output_attention_part,
        query_key_value_output_weight,
        projection_input_weight,
    ) = (
        query_key_value_whole,
        output_whole_weight,
        query_key_value_adapter_second,
        projection_adapter_first,
    )
    seen = ln1_all.shape[0]
    query_key_value_input_selected = query_key_value_adapter_first[:, head_numbers]
    qkv_out_sel = query_key_value_output_weight[:, head_numbers]
    query_key_value_middle = jnp.einsum(
        "obl,holm->hobm",
        ln1_all,
        query_key_value_input_selected,
        preferred_element_type=jnp.float32,
    )
    projected = jnp.einsum(
        "isd,djf->jisf", ln1_all, query_key_value_attention, preferred_element_type=jnp.float32
    )
    projected = projected + jnp.einsum(
        "klty,klye->klte",
        query_key_value_middle,
        qkv_out_sel.astype(jnp.float32),
        precision=highest_precision,
    )
    proj_low = projected.astype(jnp.bfloat16)
    local_width = proj_low.shape[-1]
    heads_local = local_width // HEAD_DIM
    shaped = proj_low.reshape(3, seen, length, heads_local, HEAD_DIM)
    mixed_heads, log_total = lax.map(attend_forward, (shaped[0], shaped[1], shaped[2]))
    mixed_heads = mixed_heads.reshape(seen, length, local_width)
    proj_in_sel = projection_input_weight[head_numbers]
    projection_output_selected = projection_adapter_second[head_numbers]
    projection_adapter_middle = jnp.einsum(
        "lby,lyg->lbg", mixed_heads, proj_in_sel, preferred_element_type=jnp.float32
    )
    attention_branch = jnp.einsum(
        "ise,de->isd", mixed_heads, output_attention_part, preferred_element_type=jnp.float32
    )
    attention_branch = attention_branch + jnp.einsum(
        "cmt,ctf->cmf",
        projection_adapter_middle,
        projection_output_selected.astype(jnp.float32),
        precision=highest_precision,
    )
    hidden = inputs + lax.psum_scatter(
        attention_branch.astype(jnp.bfloat16), "heads", scatter_dimension=0, tiled=True
    ).astype(jnp.float32)
    norm2, unit2, inverse2 = normalize(hidden, second_norm_gain, second_norm_bias)
    second_norm_reduced = norm2.astype(jnp.bfloat16)
    up_adapter_middle = jnp.einsum(
        "ego,eoh->egh",
        second_norm_reduced,
        up_adapter_first[owned_numbers],
        preferred_element_type=jnp.float32,
    ).astype(jnp.bfloat16)
    ln2_in, up_mid_in = (
        lax.all_gather(second_norm_reduced, "tensor", axis=0, tiled=True),
        lax.all_gather(up_adapter_middle, "tensor", axis=0, tiled=True),
    )
    up_cols, down_cols, bias_cols = (up_rows, down_rows, up_projection_bias)
    up_output_columns, down_input_columns = (up_adapter_second, down_adapter_first)
    up_input_selected = up_adapter_first[unit_numbers]
    up_out_sel = up_output_columns[unit_numbers]
    down_in_sel = down_input_columns[unit_numbers]
    down_output_selected = down_adapter_second[unit_numbers]
    residual_before = jnp.einsum(
        "isd,df->isf", ln2_in, up_cols, preferred_element_type=jnp.float32
    ) + bias_cols.astype(jnp.float32)
    residual_before = residual_before + jnp.einsum(
        "cbd,cdp->cbp",
        up_mid_in.astype(jnp.float32),
        up_out_sel.astype(jnp.float32),
        precision=highest_precision,
    )
    act_low = gelu_tanh(residual_before).astype(jnp.bfloat16)
    down_adapter_middle = jnp.einsum(
        "pco,pqo->pcq", act_low, down_in_sel, preferred_element_type=jnp.float32
    )
    mlp_part = jnp.einsum("isf,df->isd", act_low, down_cols, preferred_element_type=jnp.float32)
    mlp_part = mlp_part + jnp.einsum(
        "cmt,ctf->cmf",
        down_adapter_middle,
        down_output_selected.astype(jnp.float32),
        precision=highest_precision,
    )
    mlp_sum = lax.psum_scatter(
        mlp_part.astype(jnp.bfloat16), "tensor", scatter_dimension=0, tiled=True
    ).astype(jnp.float32)
    layer_output = hidden + mlp_sum + down_projection_bias.astype(jnp.float32)
    grad_mlp = cotangent.astype(jnp.bfloat16)
    grad_mlp_in = lax.all_gather(grad_mlp, "tensor", axis=0, tiled=True)
    grad_down_mid = jnp.einsum(
        "isd,ird->isr", grad_mlp_in, down_output_selected, preferred_element_type=jnp.float32
    )
    grad_act = jnp.einsum("isd,df->isf", grad_mlp_in, down_cols, preferred_element_type=jnp.float32)
    grad_act = grad_act + jnp.einsum(
        "cbd,cdp->cbp", grad_down_mid, down_in_sel.astype(jnp.float32), precision=highest_precision
    )
    ignored, gelu_pull = jax.vjp(gelu_tanh, residual_before)
    grad_before = gelu_pull(grad_act)[0].astype(jnp.bfloat16)
    grad_up_mid = jnp.einsum(
        "pco,pqo->pcq", grad_before, up_out_sel, preferred_element_type=jnp.float32
    )
    grad_ln2 = jnp.einsum("isf,df->isd", grad_before, up_cols, preferred_element_type=jnp.float32)
    grad_ln2 = grad_ln2 + jnp.einsum(
        "isr,idr->isd",
        grad_up_mid,
        up_input_selected.astype(jnp.float32),
        precision=highest_precision,
    )
    grad_ln2 = lax.psum_scatter(
        grad_ln2.astype(jnp.bfloat16), "tensor", scatter_dimension=0, tiled=True
    ).astype(jnp.float32)
    grad_hidden = cotangent + normalize_back(grad_ln2, unit2, inverse2, second_norm_gain)
    mlp_hot = one_hot(unit_numbers, adapter_factors)
    grad_up_in_part = by_adapter(
        mlp_hot, jnp.einsum("isd,isr->idr", ln2_in, grad_up_mid, precision=highest_precision)
    )
    grad_up_out_part = by_adapter(
        mlp_hot,
        jnp.einsum("isr,isf->irf", up_mid_in, grad_before, preferred_element_type=jnp.float32),
    )
    grad_down_in_part = by_adapter(
        mlp_hot, jnp.einsum("isr,isf->irf", grad_down_mid, act_low, precision=highest_precision)
    )
    grad_down_out_part = by_adapter(
        mlp_hot,
        jnp.einsum("isr,isd->ird", down_adapter_middle, grad_mlp_in, precision=highest_precision),
    )
    grad_branch = lax.all_gather(grad_hidden.astype(jnp.bfloat16), "heads", axis=0, tiled=True)
    grad_proj_mid = jnp.einsum(
        "isd,ird->isr", grad_branch, projection_output_selected, preferred_element_type=jnp.float32
    )
    grad_mixed = jnp.einsum(
        "isd,de->ise", grad_branch, output_attention_part, preferred_element_type=jnp.float32
    )
    grad_mixed = grad_mixed + jnp.einsum(
        "isr,ier->ise", grad_proj_mid, proj_in_sel.astype(jnp.float32), precision=highest_precision
    )
    grad_mixed = grad_mixed.astype(jnp.bfloat16).reshape(seen, length, heads_local, HEAD_DIM)
    grad_query, grad_keys, grad_values = lax.map(
        attend_back, (shaped[0], shaped[1], shaped[2], grad_mixed, log_total)
    )
    grad_proj = (
        jnp.stack([grad_query, grad_keys, grad_values])
        .reshape(3, seen, length, local_width)
        .astype(jnp.bfloat16)
    )
    grad_qkv_mid = jnp.einsum(
        "jisf,jirf->jisr", grad_proj, qkv_out_sel, preferred_element_type=jnp.float32
    )
    grad_ln1 = jnp.einsum(
        "jisf,djf->isd", grad_proj, query_key_value_attention, preferred_element_type=jnp.float32
    )
    grad_ln1 = grad_ln1 + jnp.einsum(
        "jisr,jidr->isd",
        grad_qkv_mid,
        query_key_value_input_selected.astype(jnp.float32),
        precision=highest_precision,
    )
    grad_ln1 = lax.psum_scatter(
        grad_ln1.astype(jnp.bfloat16), "heads", scatter_dimension=0, tiled=True
    ).astype(jnp.float32)
    grad_input = grad_hidden + normalize_back(grad_ln1, unit1, inverse1, first_norm_gain)
    attn_hot = one_hot(head_numbers, adapter_factors)
    qkv_in_image = jnp.einsum("isd,jisr->jidr", ln1_all, grad_qkv_mid, precision=highest_precision)
    grad_qkv_in_part = jnp.einsum(
        "ia,jidr->jadr", attn_hot, qkv_in_image, precision=highest_precision
    )
    qkv_out_image = jnp.einsum(
        "jisr,jisf->jirf", query_key_value_middle, grad_proj, precision=highest_precision
    )
    grad_qkv_out_part = jnp.einsum(
        "ia,jirf->jarf", attn_hot, qkv_out_image, precision=highest_precision
    )
    grad_proj_in_part = by_adapter(
        attn_hot,
        jnp.einsum("ise,isr->ier", mixed_heads, grad_proj_mid, precision=highest_precision),
    )
    grad_proj_out_part = by_adapter(
        attn_hot,
        jnp.einsum(
            "isr,isd->ird", projection_adapter_middle, grad_branch, precision=highest_precision
        ),
    )
    grad_qkv_in, grad_proj_out, grad_up_in, grad_down_out = lax.psum(
        (grad_qkv_in_part, grad_proj_out_part, grad_up_in_part, grad_down_out_part),
        ("fsdp", "heads", "tensor"),
    )
    grad_qkv_out, grad_proj_in = lax.psum(
        (grad_qkv_out_part, grad_proj_in_part), ("fsdp", "tensor")
    )
    grad_up_out, grad_down_in = (
        lax.psum(grad_up_out_part.astype(jnp.bfloat16), ("fsdp", "heads")).astype(jnp.float32),
        lax.psum(grad_down_in_part.astype(jnp.bfloat16), ("fsdp", "heads")).astype(jnp.float32),
    )
    return (
        layer_output,
        grad_input,
        grad_qkv_in,
        grad_qkv_out,
        grad_proj_in,
        grad_proj_out,
        grad_up_in,
        grad_up_out,
        grad_down_in,
        grad_down_out,
    )


def solution(mesh):
    in_specs = (
        P(("fsdp", "heads", "tensor"), None, None),
        P(("fsdp", "heads", "tensor"), None, None),
        P(),
        P(),
        P(),
        P(),
        P(),
        P("fsdp", None, "heads"),
        P("fsdp", "heads"),
        P("fsdp", "tensor"),
        P("fsdp", "tensor"),
        P("tensor"),
        P(),
        P(),
        P(None, None, None, "heads"),
        P(None, "heads", None),
        P(),
        P(),
        P(None, None, "tensor"),
        P(None, None, "tensor"),
        P(),
    )
    out_specs = (
        P(("fsdp", "heads", "tensor"), None, None),
        P(("fsdp", "heads", "tensor"), None, None),
        P(),
        P(None, None, None, "heads"),
        P(None, "heads", None),
        P(),
        P(),
        P(None, None, "tensor"),
        P(None, None, "tensor"),
        P(),
    )
    return jax.shard_map(
        per_device, mesh=mesh, in_specs=in_specs, out_specs=out_specs, check_vma=False
    )
```

profile of v0, /device:TPU:0, one launch (start us, length us, event | category | flops | bytes accessed | tf_op | source)
XLA Modules:
  0.0 1267.5 jit_solution(7760785568148674721)
XLA Ops:
  36.3 54.6 %all-gather.13.cloned.1.call-done = bf16[1152,3,576]{2,0,1:T(8,128)(2,1)} async-done(((bf16[288,3,576]{2,0,1:T(8,128)(2,1)}), bf16[1152,3,576]{2,0,1:T(8,128)(2,1)}) %all-gather.13.cloned.1.call-update) | async-done | bytes 3981328 | tf_op jit(solution)/shard_map/all_gather | solution.py:120
  90.9 10.7 fusion.59
  109.1 57.2 %while.28 = (s32[]{:T(128)}, bf16[2,729,8,72]{1,3,2,0:T(8,128)(2,1)}, f32[2,8,729]{2,1,0:T(8,128)S(1)}, bf16[2,729,8,72]{1,3,2,0:T(8,128)(2,1)}, bf16[2,729,8,72...) while((s32[]{:T(128)}, bf16[2,729,8,72]{1,3,2,0:T(8,128)(2,1)}, ...), condition=%wide.region_5.6_spmd, body=%wide.region_2.5_spmd.sunk | while | flops 1263117824 | bytes 55831608 | solution.py:160
  109.1 9.9 multiply_reduce_fusion.8
  119.0 9.2 fusion.206
  128.2 9.3 fusion.207
  137.5 9.9 multiply_reduce_fusion.8
  156.6 9.3 fusion.207
  202.4 102.8 %all-gather.23.cloned.1.call-done = bf16[4,729,1152]{2,1,0:T(8,128)(2,1)} async-done(((bf16[1,729,1152]{2,1,0:T(8,128)(2,1)}), bf16[4,729,1152]{2,1,0:T(8,128)(2,1)}) %all-gather.23.cloned.1.call-update) | async-done | bytes 6718480 | tf_op jit(solution)/shard_map/all_gather | solution.py:222
  310.0 34.9 %all-gather.21.cloned.1.call-done = bf16[1152,1076]{1,0:T(8,128)(2,1)} async-done(((bf16[288,1076]{1,0:T(8,128)(2,1)}), bf16[1152,1076]{1,0:T(8,128)(2,1)}) %all-gather.21.cloned.1.call-update) | async-done | bytes 2479120 | tf_op jit(solution)/shard_map/all_gather | solution.py:123
  344.9 14.5 %fusion.69 = f32[4,729,1076]{1,2,0:T(8,128)} fusion(bf16[4,729,1152]{2,1,0:T(8,128)(2,1)} %all-gather.23.cloned.1.call-done, bf16[1152,1076]{1,0:T(8,128)(2,1)} %all-gather.21.cloned.1.call-done), kind=kOutput, calls=%fused_computation.114 | convolution fusion | flops 7229067264 | bytes 21748032 | tf_op jit(solution)/shard_map/isd,df->isf/dot_general | solution.py:226
  359.9 13.3 %all-gather.1 = bf16[4,729,16]{1,2,0:T(8,128)(2,1)S(1)} all-gather(bf16[1,729,16]{1,2,0:T(8,128)(2,1)S(1)} %fusion.92), channel_id=2, replica_groups=mesh['fsdp'=4,'heads'=2,'tensor'=4] {'tensor'}, dimensions={0}, use_global_device_ids=true | all-gather | bytes 116640 | tf_op jit(solution)/shard_map/all_gather | solution.py:189
  373.2 13.1 %all-gather.19.cloned.1.call-done = bf16[1152,1076]{1,0:T(8,128)(2,1)} async-done(((bf16[288,1076]{1,0:T(8,128)(2,1)}), bf16[1152,1076]{1,0:T(8,128)(2,1)}) %all-gather.19.cloned.1.call-update) | async-done | bytes 2479120 | tf_op jit(solution)/shard_map/all_gather | solution.py:122
  386.4 124.8 %all-gather.17.cloned.1.call-done = bf16[4,729,1152]{2,1,0:T(8,128)(2,1)} async-done(((bf16[1,729,1152]{2,1,0:T(8,128)(2,1)}), bf16[4,729,1152]{2,1,0:T(8,128)(2,1)}) %all-gather.17.cloned.1.call-update) | async-done | bytes 6718480 | tf_op jit(solution)/shard_map/all_gather | solution.py:188
  511.2 12.4 fusion.75
  523.6 10.1 multiply_convert_fusion.1
  533.7 18.5 %fusion.50 = bf16[4,729,1076]{1,2,0:T(8,128)(2,1)S(1)} fusion(f32[4,729,1076]{1,2,0:T(8,128)} %get-tuple-element.204, f32[4,729,1076]{1,2,0:T(8,128)} %fusion.69, f32[4,16,729]{2,1,0:T(8,128)S(1)} %fusion.138, bf16[4,16,1076]{2,1,0:T(8,128)(2,1)S(1)} %gather_fusion.7), kind=kOutput, calls=%fused_computation.72 | convolution fusion | flops 668312192 | bytes 31700512 | tf_op jit(solution)/shard_map/cbd,cdp->cbp/dot_general | solution.py:227
  555.9 13.1 %fusion.73 = f32[4,729,1152]{2,1,0:T(8,128)} fusion(bf16[4,729,1076]{1,2,0:T(8,128)(2,1)S(1)} %fusion.50, bf16[1152,1076]{1,0:T(8,128)(2,1)S(1)} %copy-done.56), kind=kOutput, calls=%fused_computation.118 | convolution fusion | flops 7229067264 | bytes 22191264 | tf_op jit(solution)/shard_map/isf,df->isd/dot_general | solution.py:235
  569.0 10.8 add_convert_fusion
  583.9 13.5 %fusion.71 = f32[4,729,1152]{2,1,0:T(8,128)S(1)} fusion(bf16[4,729,1076]{1,2,0:T(8,128)(2,1)} %get-tuple-element.203, bf16[1152,1076]{1,0:T(8,128)(2,1)S(1)} %copy-done.55), kind=kOutput, calls=%fused_computation.116 | convolution fusion | flops 7229067264 | bytes 22191264 | tf_op jit(solution)/shard_map/isf,df->isd/dot_general | solution.py:210
  606.6 90.2 %reduce-scatter.9.cloned.1.call-done = bf16[1,729,1152]{2,1,0:T(8,128)(2,1)} async-done(((bf16[4,729,1152]{2,1,0:T(8,128)(2,1)}), bf16[1,729,1152]{2,1,0:T(8,128)(2,1)}) %reduce-scatter.9.cloned.1.call-update) | async-done | bytes 1679632 | tf_op jit(solution)/shard_map/reduce_scatter | solution.py:242
  700.4 118.0 %reduce-scatter.7.cloned.1.call-done = bf16[1,729,1152]{2,1,0:T(8,128)(2,1)} async-done(((bf16[4,729,1152]{2,1,0:T(8,128)(2,1)}), bf16[1,729,1152]{2,1,0:T(8,128)(2,1)}) %reduce-scatter.7.cloned.1.call-update) | async-done | bytes 1679632 | tf_op jit(solution)/shard_map/reduce_scatter | solution.py:217
  863.4 99.9 %while.29 = (s32[]{:T(128)}, bf16[2,729,8,72]{1,3,2,0:T(8,128)(2,1)}, bf16[2,729,8,72]{1,3,2,0:T(8,128)(2,1)}, bf16[2,729,8,72]{1,3,2,0:T(8,128)(2,1)}, bf16[2,7...) while((s32[]{:T(128)}, ...), condition=%wide.region_15.16_spmd, body=%wide.region_13.15_spmd.sunk | while | flops 3112952320 | bytes 200497152 | solution.py:272
  863.9 10.1 fusion.216
  882.1 12.7 %multiply_reduce_fusion.9 = (f32[8,729]{1,0:T(8,128)S(1)}, f32[8,729,729]{1,2,0:T(8,128)}) fusion(f32[8,729,729]{1,2,0:T(8,128)} %fusion.216, f32[8,729]{1,0:T(8,128)S(1)} %dynamic-slice_bitcast_fusion.2, bf16[2,729,8,72]{1,3,2,0:T(8,128)(2,1)S(1)} %copy-done.13, s32[]{:T(128)S(6)} %copy.187, bf16[2,729,8,72]{1,3,2,0:T(8,128)(2,1)S(1)} %copy-done.9), kind=kOutput, calls=%fused_computation.30.clone.1 | convolution fusion | flops 629220288 | bytes 35830624 | tf_op jit(solution)/shard_map/while/body/eval_jaxpr/qhd,khd->hqk/dot_general | solution.py:58
  894.8 13.2 %multiply_convert_fusion.3 = bf16[8,729,729]{1,2,0:T(8,128)(2,1)S(1)} fusion(f32[8,729,729]{1,2,0:T(8,128)} %get-tuple-element.305, f32[8,729,729]{1,2,0:T(8,128)} %fusion.216, f32[8,729]{1,0:T(8,128)S(1)} %get-tuple-element.306, f32[8,729]{1,0:T(8,128)S(1)} %dynamic-slice_bitcast_fusion.2), kind=kLoop, calls=%fused_computation.29.clone.1 | loop fusion | flops 21257640 | bytes 42561936 | tf_op jit(solution)/shard_map/while/body/eval_jaxpr/convert_element_type | solution.py:63
  913.8 10.0 fusion.216
  932.0 12.6 multiply_reduce_fusion.9
  944.5 13.1 %multiply_convert_fusion.3 = bf16[8,729,729]{1,2,0:T(8,128)(2,1)S(1)} fusion(f32[8,729,729]{1,2,0:T(8,128)} %get-tuple-element.305, f32[8,729,729]{1,2,0:T(8,128)} %fusion.216, f32[8,729]{1,0:T(8,128)S(1)} %get-tuple-element.306, f32[8,729]{1,0:T(8,128)S(1)} %dynamic-slice_bitcast_fusion.2), kind=kLoop, calls=%fused_computation.29.clone.1 | loop fusion | flops 21257640 | bytes 42561936 | tf_op jit(solution)/shard_map/while/body/eval_jaxpr/convert_element_type | solution.py:63
  983.7 11.9 fusion.57
  1011.3 76.5 %all-reduce.9.cloned.1.call-done = (f32[3,8,16,576]{3,1,2,0:T(8,128)}, f32[8,576,16]{1,0,2:T(8,128)}) async-done(((f32[3,8,16,576]{3,1,2,0:T(8,128)}, f32[8,576,16]{1,0,2:T(8,128)}), (f32[3,8,16,576]{3,1,2,0:T(8,128)}, f32[8,576,16]{1,0,2:T(8,128)})) %all-reduce.9.cloned.1.call-update) | async-done | bytes 1179664 | tf_op jit(solution)/shard_map/psum | solution.py:321
  1091.8 142.8 %all-reduce.7.cloned.1.call-done = (f32[3,8,1152,16]{2,1,3,0:T(8,128)}, f32[8,16,1152]{2,0,1:T(8,128)}, f32[8,1152,16]{1,0,2:T(8,128)}, f32[8,16,1152]{2,0,1:T(8,128)}) async-done(((f32[3,8,1152,16]{2,1,3,0:T(8,128)}, f32[8,16,1152]{2,0,1:T(8,128)}, f32[8,1152,16]{1,0,2:T(8,128)}, f32[8,16,1152]{2,0,1:T(8,128)}), (f32[3,8,1152,16]{2,1,3,0:T(8,128)}, f32[8,16,1152]{2,0,1:T(8,128)}, f32[8,1152,16]{1,0,2:T(8,128)}, ...) | async-done | bytes 3538960 | tf_op jit(solution)/shard_map/psum | solution.py:317
  (288 shorter events, 242.4 us)
Async XLA Ops:
  8.0 17.2 %copy-start = (bf16[3,8,1152,16]{2,3,1,0:T(8,128)(2,1)S(1)}, bf16[3,8,1152,16]{2,3,1,0:T(8,128)(2,1)}, u32[]{:S(2)}) copy-start(bf16[3,8,1152,16]{2,3,1,0:T(8,128)(2,1)} %param.38) | copy-start | bytes 2654212
  8.0 25.2 %all-gather.11.cloned.1.call-start = ((), (), s32[]{:S(2)}) async-start(), calls=%async_computation.4 | async-start | bytes 5087232 | tf_op jit(solution)/shard_map/all_gather | solution.py:126
  17.9 73.0 %all-gather.13.cloned.1.call-start = ((), (), s32[]{:S(2)}) async-start(), calls=%async_computation.5 | async-start | bytes 5529600 | tf_op jit(solution)/shard_map/all_gather | solution.py:120
  18.6 150.3 %all-gather.15.cloned.1.call-start = ((), (), s32[]{:S(2)}) async-start(), calls=%async_computation.6 | async-start | bytes 1843200 | tf_op jit(solution)/shard_map/all_gather | solution.py:121
  19.4 170.4 %reduce-scatter.5.cloned.1.call-start = ((), (), s32[]{:S(2)}) async-start(), calls=%async_computation.7 | async-start | bytes 5087232 | tf_op jit(solution)/shard_map/reduce_scatter | solution.py:176
  25.2 76.4 %copy-start.32 = (bf16[2,3,16,576]{3,2,1,0:T(8,128)(2,1)}, bf16[2,3,16,576]{3,2,1,0:T(8,128)(2,1)S(1)}, u32[]{:S(2)}) copy-start(bf16[2,3,16,576]{3,2,1,0:T(8,128)(2,1)S(1)} %gather_fusion.2) | copy-start | bytes 331780
  25.8 75.8 %copy-start.11 = (bf16[2,3,1152,16]{2,3,1,0:T(8,128)(2,1)}, bf16[2,3,1152,16]{2,3,1,0:T(8,128)(2,1)S(1)}, u32[]{:S(2)}) copy-start(bf16[2,3,1152,16]{2,3,1,0:T(8,128)(2,1)S(1)} %gather_fusion.1) | copy-start | bytes 663556
  36.3 65.4 %copy-start.25 = (f32[3,2,729,16]{2,3,0,1:T(8,128)}, f32[3,2,729,16]{2,3,0,1:T(8,128)S(1)}, u32[]{:S(2)}) copy-start(f32[3,2,729,16]{2,3,0,1:T(8,128)S(1)} %fusion.86) | copy-start | bytes 839812
  109.1 57.2 %copy-start.21 = (bf16[2,576,16]{1,2,0:T(8,128)(2,1)S(1)}, bf16[2,576,16]{1,2,0:T(8,128)(2,1)}, u32[]{:S(2)}) copy-start(bf16[2,576,16]{1,2,0:T(8,128)(2,1)} %gather_fusion.3) | copy-start | bytes 110596
  178.4 126.8 %all-gather.23.cloned.1.call-start = ((), (), s32[]{:S(2)}) async-start(), calls=%async_computation.12 | async-start | bytes 8478720 | tf_op jit(solution)/shard_map/all_gather | solution.py:222
  181.8 163.1 %all-gather.21.cloned.1.call-start = ((), (), s32[]{:S(2)}) async-start(), calls=%async_computation.10 | async-start | bytes 3317760 | tf_op jit(solution)/shard_map/all_gather | solution.py:123
  182.4 204.0 %all-gather.19.cloned.1.call-start = ((), (), s32[]{:S(2)}) async-start(), calls=%async_computation.9 | async-start | bytes 3317760 | tf_op jit(solution)/shard_map/all_gather | solution.py:122
  182.9 328.3 %all-gather.17.cloned.1.call-start = ((), (), s32[]{:S(2)}) async-start(), calls=%async_computation.8 | async-start | bytes 8478720 | tf_op jit(solution)/shard_map/all_gather | solution.py:188
  196.7 500.0 %reduce-scatter.9.cloned.1.call-start = ((), (), s32[]{:S(2)}) async-start(), calls=%async_computation.13 | async-start | bytes 8478720 | tf_op jit(solution)/shard_map/reduce_scatter | solution.py:242
  310.0 49.4 %copy-start.14 = (bf16[1,729,1152]{2,1,0:T(8,128)(2,1)S(1)}, bf16[1,729,1152]{2,1,0:T(8,128)(2,1)}, u32[]{:S(2)}) copy-start(bf16[1,729,1152]{2,1,0:T(8,128)(2,1)} %add_convert_fusion.4) | copy-start | bytes 5038852
  373.2 150.3 %copy-start.34 = (bf16[4,729,16]{1,2,0:T(8,128)(2,1)}, bf16[4,729,16]{1,2,0:T(8,128)(2,1)S(1)}, u32[]{:S(2)}) copy-start(bf16[4,729,16]{1,2,0:T(8,128)(2,1)S(1)} %all-gather.1) | copy-start | bytes 279940
  579.8 238.6 %reduce-scatter.7.cloned.1.call-start = ((), (), s32[]{:S(2)}) async-start(), calls=%async_computation.11 | async-start | bytes 8478720 | tf_op jit(solution)/shard_map/reduce_scatter | solution.py:217
  605.9 245.4 %all-gather.25.cloned.1.call-start = ((), (), s32[]{:S(2)}) async-start(), calls=%async_computation.14 | async-start | bytes 5087232 | tf_op jit(solution)/shard_map/all_gather | solution.py:261
  696.8 121.6 %copy-start.18 = (bf16[1,729,1152]{2,1,0:T(8,128)(2,1)S(1)}, bf16[1,729,1152]{2,1,0:T(8,128)(2,1)}, u32[]{:S(2)}) copy-start(bf16[1,729,1152]{2,1,0:T(8,128)(2,1)} %reduce-scatter.9.cloned.1.call-done) | copy-start | bytes 5038852
  824.8 175.7 %all-reduce.11.cloned.1.call-start = ((), (), s32[]{:S(2)}) async-start(), calls=%async_computation.18 | async-start | bytes 1179648 | tf_op jit(solution)/shard_map/psum | solution.py:325
  833.7 13.3 %slice-start = ((s8[6782976]{0:T(1024)(128)(4,1)}), s8[2588672]{0:T(1024)(128)(4,1)S(1)}, s32[]{:S(2)}) async-start(s8[6782976]{0:T(1024)(128)(4,1)} %bitcast.261), calls=%async_computation.19 | async-start | bytes 5177344
  851.2 236.6 %all-reduce.9.cloned.1.call-start = ((), (), s32[]{:S(2)}) async-start(), calls=%async_computation.17 | async-start | bytes 2621440 | tf_op jit(solution)/shard_map/psum | solution.py:321
  863.4 99.9 %copy-start.26 = (f32[3,2,729,16]{2,3,0,1:T(8,128)S(1)}, f32[3,2,729,16]{2,3,0,1:T(8,128)}, u32[]{:S(2)}) copy-start(f32[3,2,729,16]{2,3,0,1:T(8,128)} %copy-done.25) | copy-start | bytes 839812
  894.8 13.3 %copy-start.6 = (bf16[2,729,8,72]{1,3,2,0:T(8,128)(2,1)S(1)}, bf16[2,729,8,72]{1,3,2,0:T(8,128)(2,1)}, u32[]{:S(2)}) copy-start(bf16[2,729,8,72]{1,3,2,0:T(8,128)(2,1)} %get-tuple-element.353) | copy-start | bytes 5038852 | tf_op jit(solution)/shard_map/while
  894.8 13.3 %copy-start.60 = (bf16[2,729,8,72]{1,3,2,0:T(8,128)(2,1)S(1)}, bf16[2,729,8,72]{1,3,2,0:T(8,128)(2,1)}, u32[]{:S(2)}) copy-start(bf16[2,729,8,72]{1,3,2,0:T(8,128)(2,1)} %get-tuple-element.340) | copy-start | bytes 5038852 | tf_op jit(solution)/shard_map/while
  944.5 13.1 %copy-start.6 = (bf16[2,729,8,72]{1,3,2,0:T(8,128)(2,1)S(1)}, bf16[2,729,8,72]{1,3,2,0:T(8,128)(2,1)}, u32[]{:S(2)}) copy-start(bf16[2,729,8,72]{1,3,2,0:T(8,128)(2,1)} %get-tuple-element.353) | copy-start | bytes 5038852 | tf_op jit(solution)/shard_map/while
  944.5 13.1 %copy-start.60 = (bf16[2,729,8,72]{1,3,2,0:T(8,128)(2,1)S(1)}, bf16[2,729,8,72]{1,3,2,0:T(8,128)(2,1)}, u32[]{:S(2)}) copy-start(bf16[2,729,8,72]{1,3,2,0:T(8,128)(2,1)} %get-tuple-element.340) | copy-start | bytes 5038852 | tf_op jit(solution)/shard_map/while
  972.4 262.2 %all-reduce.7.cloned.1.call-start = ((), (), s32[]{:S(2)}) async-start(), calls=%async_computation.16 | async-start | bytes 7077888 | tf_op jit(solution)/shard_map/psum | solution.py:317
  983.7 263.7 %reduce-scatter.11.cloned.1.call-start = ((), (), s32[]{:S(2)}) async-start(), calls=%async_computation.15 | async-start | bytes 5087232 | tf_op jit(solution)/shard_map/reduce_scatter | solution.py:292
  1234.6 12.7 %copy-start.40 = (f32[729]{0:T(1024)S(1)}, f32[729]{0:T(1024)}, u32[]{:S(2)}) copy-start(f32[729]{0:T(1024)} %copy-done.39) | copy-start | bytes 8752
  1234.6 12.7 %copy-start.43 = (f32[1152]{0:T(1024)S(1)}, f32[1152]{0:T(1024)}, u32[]{:S(2)}) copy-start(f32[1152]{0:T(1024)} %param.28) | copy-start | bytes 13828
  1234.7 12.7 %copy-start.48 = (f32[729]{0:T(1024)S(1)}, f32[729]{0:T(1024)}, u32[]{:S(2)}) copy-start(f32[729]{0:T(1024)} %copy-done.47) | copy-start | bytes 8752
  (60 other events, 316.2 us)
Sparse Core Ops, SparseCore 0:
  18.0 15.1 all-gather.10
  35.0 55.7 all-gather.12
  92.7 30.1 all-gather.14
  178.5 11.2 reduce-scatter.4
  824.9 12.9 all-gather.24
  851.3 55.7 all-reduce.10
  972.6 115.1 all-reduce.8
  1094.9 139.7 all-reduce.6
  1237.0 10.2 reduce-scatter.10
Sparse Core Ops, SparseCore 1:
  181.9 123.2 all-gather.22
  306.9 37.9 all-gather.20
  346.6 39.7 all-gather.18
  387.9 123.2 all-gather.16
  579.9 116.8 reduce-scatter.8
  699.2 119.1 reduce-scatter.6
where the time goes:
time: 1270 us
  waiting for transfers between devices  781 us (61%)
  matrix products  326 us (26%)
  other arithmetic  77 us (6%)
  local copies, waits for them, and re-layouts  49.9 us (4%)
  between operations  18.4 us (1%)
  blocking collectives  13.3 us (1%)
    psum x1, waiting for transfers between devices, per_device(): lax.psum((grad_qkv_in_part, grad_proj_out_part, grad_up_in_part, grad_dow...  143 us
    all_gather x1, waiting for transfers between devices, per_device(): lax.all_gather(second_norm_reduced, 'tensor', axis=0, tiled=True)  125 us
    reduce_scatter x1, waiting for transfers between devices, per_device(): lax.psum_scatter(mlp_part.astype(jnp.bfloat16), 'tensor', scatter_dimensi...  118 us
    all_gather x1, waiting for transfers between devices, per_device(): grad_mlp_in = lax.all_gather(grad_mlp, 'tensor', axis=0, tiled=True)  103 us
    reduce_scatter x1, waiting for transfers between devices, per_device(): lax.psum_scatter(grad_ln2.astype(jnp.bfloat16), 'tensor', scatter_dimensi...  90.2 us
    psum x1, waiting for transfers between devices, per_device(): lax.psum((grad_qkv_out_part, grad_proj_in_part), ('fsdp', 'tensor'))  76.5 us
    all_gather x1, waiting for transfers between devices, per_device(): lax.all_gather(query_key_value_weight, 'fsdp', axis=0, tiled=True)  54.6 us
    unnamed x129, local copies, waits for them, and re-layouts  35.5 us
  transfers between devices with their start and end apart: 15, of which 12 were waited for; matrix products, arithmetic and copies ran while one was open for 27% of the time, Pallas kernels for 0%

commit v1 on v0

--- a/solution.py
+++ b/solution.py
@@ -6,6 +6,17 @@
 HEAD_DIM = 72
 highest_precision = lax.Precision.HIGHEST
 norm_eps = 1e-06
+
+
+def ring_gather(x, axis, dim):
+    ways = lax.axis_size(axis)
+    pieces = [x]
+    for far in range(1, ways):
+        pieces.append(
+            lax.ppermute(pieces[far - 1], axis, [(d, (d - 1) % ways) for d in range(ways)])
+        )
+    line = jnp.concatenate(pieces, axis=dim)
+    return jnp.roll(line, lax.axis_index(axis) * x.shape[dim], axis=dim)
 
 
 def normalize(values, gain, bias):
@@ -185,7 +196,7 @@
         preferred_element_type=jnp.float32,
     ).astype(jnp.bfloat16)
     ln2_in, up_mid_in = (
-        lax.all_gather(second_norm_reduced, "tensor", axis=0, tiled=True),
+        ring_gather(second_norm_reduced, "tensor", 0),
         lax.all_gather(up_adapter_middle, "tensor", axis=0, tiled=True),
     )
     up_cols, down_cols, bias_cols = (up_rows, down_rows, up_projection_bias)

time: 1270 us -> 1230 us (0.969)
  waiting for transfers between devices: 781 us -> 685 us
  blocking collectives: 13.3 us -> 42.7 us
  local copies, waits for them, and re-layouts: 49.9 us -> 65 us
    all_gather x1 -> x0, waiting for transfers between devices: 125 us -> none  [per_device(): lax.all_gather(second_norm_reduced, 'tensor', axis=0, tiled=True)]
    all_gather x1, waiting for transfers between devices: 103 us -> 146 us  [per_device(): grad_mlp_in = lax.all_gather(grad_mlp, 'tensor', axis=0, tiled=True)]
    all_gather x1, waiting for transfers between devices: 34.9 us -> 0.01 us  [per_device(): lax.all_gather(down_weight, 'fsdp', axis=0, tiled=True)]
    ppermute x0 -> x3, waiting for transfers between devices: none -> 30.1 us  [ring_gather(): lax.ppermute(pieces[far - 1], axis, [(d, (d - 1) % ways) for d in range(w...]
    all_gather x1, blocking collectives: 13.3 us -> 42.7 us  [per_device(): lax.all_gather(up_adapter_middle, 'tensor', axis=0, tiled=True)]
    all_gather x1, waiting for transfers between devices: 13.1 us -> 0.01 us  [per_device(): lax.all_gather(up_weight, 'fsdp', axis=0, tiled=True)]
    unnamed x129, local copies, waits for them, and re-layouts: 35.5 us -> 48.4 us
  transfers between devices with their start and end apart: 15 -> 17, of which waited for: 12 -> 10; matrix products, arithmetic and copies ran while one was open for 27% -> 29% of each run, Pallas kernels for 0% -> 0%
where the time goes in v1:
time: 1230 us
  waiting for transfers between devices  685 us (56%)
  matrix products  328 us (27%)
  other arithmetic  76.6 us (6%)
  local copies, waits for them, and re-layouts  65 us (5%)
  blocking collectives  42.7 us (3%)
  between operations  17 us (1%)
  starting transfers between devices  13.2 us (1%)
    all_gather x1, waiting for transfers between devices, per_device(): grad_mlp_in = lax.all_gather(grad_mlp, 'tensor', axis=0, tiled=True)  146 us
    psum x1, waiting for transfers between devices, per_device(): lax.psum((grad_qkv_in_part, grad_proj_out_part, grad_up_in_part, grad_dow...  143 us
    reduce_scatter x1, waiting for transfers between devices, per_device(): lax.psum_scatter(mlp_part.astype(jnp.bfloat16), 'tensor', scatter_dimensi...  118 us
    reduce_scatter x1, waiting for transfers between devices, per_device(): lax.psum_scatter(grad_ln2.astype(jnp.bfloat16), 'tensor', scatter_dimensi...  93.7 us
    psum x1, waiting for transfers between devices, per_device(): lax.psum((grad_qkv_out_part, grad_proj_in_part), ('fsdp', 'tensor'))  76.4 us
    all_gather x1, waiting for transfers between devices, per_device(): lax.all_gather(query_key_value_weight, 'fsdp', axis=0, tiled=True)  54.6 us
    unnamed x129, local copies, waits for them, and re-layouts  48.4 us
    all_gather x1, blocking collectives, per_device(): lax.all_gather(up_adapter_middle, 'tensor', axis=0, tiled=True)  42.7 us
  transfers between devices with their start and end apart: 17, of which 10 were waited for; matrix products, arithmetic and copies ran while one was open for 29% of the time, Pallas kernels for 0%

profile of v1, /device:TPU:0, one launch (start us, length us, event | category | flops | bytes accessed | tf_op | source)
XLA Modules:
  0.0 1228.6 jit_solution(9868067713363396942)
XLA Ops:
  35.4 54.6 %all-gather.12.cloned.1.call-done = bf16[1152,3,576]{2,0,1:T(8,128)(2,1)} async-done(((bf16[288,3,576]{2,0,1:T(8,128)(2,1)}), bf16[1152,3,576]{2,0,1:T(8,128)(2,1)}) %all-gather.12.cloned.1.call-update) | async-done | bytes 3981328 | tf_op jit(solution)/shard_map/all_gather | solution.py:131
  90.0 10.7 fusion.62
  108.3 57.2 %while.28 = (s32[]{:T(128)}, bf16[2,729,8,72]{1,3,2,0:T(8,128)(2,1)}, f32[2,8,729]{2,1,0:T(8,128)S(1)}, bf16[2,729,8,72]{1,3,2,0:T(8,128)(2,1)}, bf16[2,729,8,72...) while((s32[]{:T(128)}, bf16[2,729,8,72]{1,3,2,0:T(8,128)(2,1)}, ...), condition=%wide.region_5.6_spmd, body=%wide.region_2.5_spmd.sunk | while | flops 1263117824 | bytes 55831608 | solution.py:171
  108.3 9.9 multiply_reduce_fusion.8
  118.2 9.2 fusion.208
  127.4 9.3 fusion.209
  136.7 9.9 multiply_reduce_fusion.8
  146.5 9.2 fusion.208
  155.7 9.3 fusion.209
  204.7 30.1 %collective-permute-done = bf16[1,729,1152]{2,1,0:T(8,128)(2,1)} collective-permute-done((bf16[1,729,1152]{2,1,0:T(8,128)(2,1)S(1)}, bf16[1,729,1152]{2,1,0:T(8,128)(2,1)}, u32[]{:S(2)}, u32[]{:S(2)}) %collective-permute-start) | collective-permute-done | bytes 1679648 | tf_op jit(solution)/shard_map/ppermute | solution.py:16
  239.2 145.7 %all-gather.20.cloned.1.call-done = bf16[4,729,1152]{2,1,0:T(8,128)(2,1)} async-done(((bf16[1,729,1152]{2,1,0:T(8,128)(2,1)}), bf16[4,729,1152]{2,1,0:T(8,128)(2,1)}) %all-gather.20.cloned.1.call-update) | async-done | bytes 6718480 | tf_op jit(solution)/shard_map/all_gather | solution.py:233
  384.9 14.8 %fusion.72 = f32[4,729,1076]{1,2,0:T(8,128)} fusion(bf16[4,729,1152]{2,1,0:T(8,128)(2,1)} %all-gather.20.cloned.1.call-done, bf16[1152,1076]{1,0:T(8,128)(2,1)} %all-gather.18.cloned.1.call-done), kind=kOutput, calls=%fused_computation.117 | convolution fusion | flops 7229067264 | bytes 21748032 | tf_op jit(solution)/shard_map/isd,df->isf/dot_general | solution.py:237
  406.8 42.7 %all-gather.1 = bf16[4,729,16]{1,2,0:T(8,128)(2,1)S(1)} all-gather(bf16[1,729,16]{1,2,0:T(8,128)(2,1)S(1)} %fusion.94), channel_id=2, replica_groups=mesh['fsdp'=4,'heads'=2,'tensor'=4] {'tensor'}, dimensions={0}, use_global_device_ids=true | all-gather | bytes 116640 | tf_op jit(solution)/shard_map/all_gather | solution.py:200
  471.4 21.2 %multiply_convert_fusion.1 = (bf16[4,729,1076]{1,2,0:T(8,128)(2,1)}, f32[4,729,1076]{1,2,0:T(8,128)}) fusion(f32[4,729,1076]{1,2,0:T(8,128)} %fusion.141, f32[1076]{0:T(1024)S(1)} %convert_element_type.104, bf16[1152,1076]{1,0:T(8,128)(2,1)} %all-gather.16.cloned.1.call-done, bf16[8,729,1152]{2,1,0:T(8,128)(2,1)} %constant_dynamic-update-slice_fusion, ...), kind=kOutput, calls=%fused_computation.73 | convolution fusion | flops 7263580160 | bytes 41538228 | tf_op jit(solution)/shard_map/isd,df->isf/dot_general | solution.py:208
  492.6 18.5 %fusion.50 = bf16[4,729,1076]{1,2,0:T(8,128)(2,1)S(1)} fusion(f32[4,729,1076]{1,2,0:T(8,128)} %get-tuple-element.206, f32[4,729,1076]{1,2,0:T(8,128)} %fusion.72, f32[4,16,729]{2,1,0:T(8,128)S(1)} %fusion.143, bf16[4,16,1076]{2,1,0:T(8,128)(2,1)S(1)} %gather_fusion.7), kind=kOutput, calls=%fused_computation.72 | convolution fusion | flops 668312192 | bytes 31700512 | tf_op jit(solution)/shard_map/cbd,cdp->cbp/dot_general | solution.py:238
  514.8 13.2 %fusion.76 = f32[4,729,1152]{2,1,0:T(8,128)} fusion(bf16[4,729,1076]{1,2,0:T(8,128)(2,1)S(1)} %fusion.50, bf16[1152,1076]{1,0:T(8,128)(2,1)S(1)} %copy-done.53), kind=kOutput, calls=%fused_computation.121 | convolution fusion | flops 7229067264 | bytes 22191264 | tf_op jit(solution)/shard_map/isf,df->isd/dot_general | solution.py:246
  528.0 10.8 add_convert_fusion
  542.9 12.9 %fusion.74 = f32[4,729,1152]{2,1,0:T(8,128)S(1)} fusion(bf16[4,729,1076]{1,2,0:T(8,128)(2,1)} %get-tuple-element.205, bf16[1152,1076]{1,0:T(8,128)(2,1)S(1)} %copy-done.52), kind=kOutput, calls=%fused_computation.119 | convolution fusion | flops 7229067264 | bytes 22191264 | tf_op jit(solution)/shard_map/isf,df->isd/dot_general | solution.py:221
  555.7 8.5 add_convert_fusion.1
  565.0 93.7 %reduce-scatter.9.cloned.1.call-done = bf16[1,729,1152]{2,1,0:T(8,128)(2,1)} async-done(((bf16[4,729,1152]{2,1,0:T(8,128)(2,1)}), bf16[1,729,1152]{2,1,0:T(8,128)(2,1)}) %reduce-scatter.9.cloned.1.call-update) | async-done | bytes 1679632 | tf_op jit(solution)/shard_map/reduce_scatter | solution.py:253
  662.4 118.0 %reduce-scatter.7.cloned.1.call-done = bf16[1,729,1152]{2,1,0:T(8,128)(2,1)} async-done(((bf16[4,729,1152]{2,1,0:T(8,128)(2,1)}), bf16[1,729,1152]{2,1,0:T(8,128)(2,1)}) %reduce-scatter.7.cloned.1.call-update) | async-done | bytes 1679632 | tf_op jit(solution)/shard_map/reduce_scatter | solution.py:228
  825.4 99.8 %while.29 = (s32[]{:T(128)}, bf16[2,729,8,72]{1,3,2,0:T(8,128)(2,1)}, bf16[2,729,8,72]{1,3,2,0:T(8,128)(2,1)}, bf16[2,729,8,72]{1,3,2,0:T(8,128)(2,1)}, bf16[2,7...) while((s32[]{:T(128)}, ...), condition=%wide.region_15.16_spmd, body=%wide.region_13.15_spmd.sunk | while | flops 3112952320 | bytes 200497152 | solution.py:283
  825.9 10.0 fusion.218
  835.9 8.1 bitcast_dynamic-update-slice_fusion.11
  844.1 12.7 %multiply_reduce_fusion.9 = (f32[8,729]{1,0:T(8,128)S(1)}, f32[8,729,729]{1,2,0:T(8,128)}) fusion(f32[8,729,729]{1,2,0:T(8,128)} %fusion.218, f32[8,729]{1,0:T(8,128)S(1)} %dynamic-slice_bitcast_fusion.2, bf16[2,729,8,72]{1,3,2,0:T(8,128)(2,1)S(1)} %copy-done.14, s32[]{:T(128)S(6)} %copy.194, bf16[2,729,8,72]{1,3,2,0:T(8,128)(2,1)S(1)} %copy-done.9), kind=kOutput, calls=%fused_computation.30.clone.1 | convolution fusion | flops 629220288 | bytes 35830624 | tf_op jit(solution)/shard_map/while/body/eval_jaxpr/qhd,khd->hqk/dot_general | solution.py:69
  856.8 13.2 %multiply_convert_fusion.3 = bf16[8,729,729]{1,2,0:T(8,128)(2,1)S(1)} fusion(f32[8,729,729]{1,2,0:T(8,128)} %get-tuple-element.307, f32[8,729,729]{1,2,0:T(8,128)} %fusion.218, f32[8,729]{1,0:T(8,128)S(1)} %get-tuple-element.308, f32[8,729]{1,0:T(8,128)S(1)} %dynamic-slice_bitcast_fusion.2), kind=kLoop, calls=%fused_computation.29.clone.1 | loop fusion | flops 21257640 | bytes 42561936 | tf_op jit(solution)/shard_map/while/body/eval_jaxpr/convert_element_type | solution.py:74
  875.7 10.0 fusion.218
  893.9 12.6 %multiply_reduce_fusion.9 = (f32[8,729]{1,0:T(8,128)S(1)}, f32[8,729,729]{1,2,0:T(8,128)}) fusion(f32[8,729,729]{1,2,0:T(8,128)} %fusion.218, f32[8,729]{1,0:T(8,128)S(1)} %dynamic-slice_bitcast_fusion.2, bf16[2,729,8,72]{1,3,2,0:T(8,128)(2,1)S(1)} %copy-done.14, s32[]{:T(128)S(6)} %copy.194, bf16[2,729,8,72]{1,3,2,0:T(8,128)(2,1)S(1)} %copy-done.9), kind=kOutput, calls=%fused_computation.30.clone.1 | convolution fusion | flops 629220288 | bytes 35830624 | tf_op jit(solution)/shard_map/while/body/eval_jaxpr/qhd,khd->hqk/dot_general | solution.py:69
  906.5 13.1 %multiply_convert_fusion.3 = bf16[8,729,729]{1,2,0:T(8,128)(2,1)S(1)} fusion(f32[8,729,729]{1,2,0:T(8,128)} %get-tuple-element.307, f32[8,729,729]{1,2,0:T(8,128)} %fusion.218, f32[8,729]{1,0:T(8,128)S(1)} %get-tuple-element.308, f32[8,729]{1,0:T(8,128)S(1)} %dynamic-slice_bitcast_fusion.2), kind=kLoop, calls=%fused_computation.29.clone.1 | loop fusion | flops 21257640 | bytes 42561936 | tf_op jit(solution)/shard_map/while/body/eval_jaxpr/convert_element_type | solution.py:74
  945.6 11.9 fusion.60
  973.2 76.4 %all-reduce.9.cloned.1.call-done = (f32[3,8,16,576]{3,1,2,0:T(8,128)}, f32[8,576,16]{1,0,2:T(8,128)}) async-done(((f32[3,8,16,576]{3,1,2,0:T(8,128)}, f32[8,576,16]{1,0,2:T(8,128)}), (f32[3,8,16,576]{3,1,2,0:T(8,128)}, f32[8,576,16]{1,0,2:T(8,128)})) %all-reduce.9.cloned.1.call-update) | async-done | bytes 1179664 | tf_op jit(solution)/shard_map/psum | solution.py:332
  1053.8 142.8 %all-reduce.7.cloned.1.call-done = (f32[3,8,1152,16]{2,1,3,0:T(8,128)}, f32[8,16,1152]{2,0,1:T(8,128)}, f32[8,1152,16]{1,0,2:T(8,128)}, f32[8,16,1152]{2,0,1:T(8,128)}) async-done(((f32[3,8,1152,16]{2,1,3,0:T(8,128)}, f32[8,16,1152]{2,0,1:T(8,128)}, f32[8,1152,16]{1,0,2:T(8,128)}, f32[8,16,1152]{2,0,1:T(8,128)}), (f32[3,8,1152,16]{2,1,3,0:T(8,128)}, f32[8,16,1152]{2,0,1:T(8,128)}, f32[8,1152,16]{1,0,2:T(8,128)}, ...) | async-done | bytes 3538960 | tf_op jit(solution)/shard_map/psum | solution.py:328
  (292 shorter events, 247.5 us)
Async XLA Ops:
  7.2 17.2 %copy-start = (bf16[3,8,1152,16]{2,3,1,0:T(8,128)(2,1)S(1)}, bf16[3,8,1152,16]{2,3,1,0:T(8,128)(2,1)}, u32[]{:S(2)}) copy-start(bf16[3,8,1152,16]{2,3,1,0:T(8,128)(2,1)} %param.38) | copy-start | bytes 2654212
  7.2 25.2 %all-gather.10.cloned.1.call-start = ((), (), s32[]{:S(2)}) async-start(), calls=%async_computation.4 | async-start | bytes 5087232 | tf_op jit(solution)/shard_map/all_gather | solution.py:137
  17.0 73.0 %all-gather.12.cloned.1.call-start = ((), (), s32[]{:S(2)}) async-start(), calls=%async_computation.5 | async-start | bytes 5529600 | tf_op jit(solution)/shard_map/all_gather | solution.py:131
  17.8 150.2 %all-gather.14.cloned.1.call-start = ((), (), s32[]{:S(2)}) async-start(), calls=%async_computation.6 | async-start | bytes 1843200 | tf_op jit(solution)/shard_map/all_gather | solution.py:132
  18.5 170.4 %reduce-scatter.5.cloned.1.call-start = ((), (), s32[]{:S(2)}) async-start(), calls=%async_computation.7 | async-start | bytes 5087232 | tf_op jit(solution)/shard_map/reduce_scatter | solution.py:187
  24.4 76.4 %copy-start.32 = (bf16[2,3,16,576]{3,2,1,0:T(8,128)(2,1)}, bf16[2,3,16,576]{3,2,1,0:T(8,128)(2,1)S(1)}, u32[]{:S(2)}) copy-start(bf16[2,3,16,576]{3,2,1,0:T(8,128)(2,1)S(1)} %gather_fusion.2) | copy-start | bytes 331780
  25.0 75.8 %copy-start.12 = (bf16[2,3,1152,16]{2,3,1,0:T(8,128)(2,1)}, bf16[2,3,1152,16]{2,3,1,0:T(8,128)(2,1)S(1)}, u32[]{:S(2)}) copy-start(bf16[2,3,1152,16]{2,3,1,0:T(8,128)(2,1)S(1)} %gather_fusion.1) | copy-start | bytes 663556
  35.4 65.4 %copy-start.25 = (f32[3,2,729,16]{2,3,0,1:T(8,128)}, f32[3,2,729,16]{2,3,0,1:T(8,128)S(1)}, u32[]{:S(2)}) copy-start(f32[3,2,729,16]{2,3,0,1:T(8,128)S(1)} %fusion.88) | copy-start | bytes 839812
  108.3 57.2 %copy-start.21 = (bf16[2,576,16]{1,2,0:T(8,128)(2,1)S(1)}, bf16[2,576,16]{1,2,0:T(8,128)(2,1)}, u32[]{:S(2)}) copy-start(bf16[2,576,16]{1,2,0:T(8,128)(2,1)} %gather_fusion.3) | copy-start | bytes 110596
  177.5 61.7 %all-gather.18.cloned.1.call-start = ((), (), s32[]{:S(2)}) async-start(), calls=%async_computation.9 | async-start | bytes 3317760 | tf_op jit(solution)/shard_map/all_gather | solution.py:134
  178.1 206.8 %all-gather.20.cloned.1.call-start = ((), (), s32[]{:S(2)}) async-start(), calls=%async_computation.11 | async-start | bytes 8478720 | tf_op jit(solution)/shard_map/all_gather | solution.py:233
  181.5 289.8 %all-gather.16.cloned.1.call-start = ((), (), s32[]{:S(2)}) async-start(), calls=%async_computation.8 | async-start | bytes 3317760 | tf_op jit(solution)/shard_map/all_gather | solution.py:133
  194.5 40.3 %collective-permute-start = (bf16[1,729,1152]{2,1,0:T(8,128)(2,1)S(1)}, bf16[1,729,1152]{2,1,0:T(8,128)(2,1)}, u32[]{:S(2)}, u32[]{:S(2)}) collective-permute-start(bf16[1,729,1152]{2,1,0:T(8,128)(2,1)S(1)} %get-tuple-element.194), channel_id=1, source_target_pairs={{0,3},{1,0},{2,1},{3,2},{4,7},{5,4},{6,5},{7,6},{8,11},{9,8},{10,9... | collective-permute-start | bytes 5038856 | tf_op jit(solution)/shard_map/ppermute | solution.py:16
  198.1 460.6 %reduce-scatter.9.cloned.1.call-start = ((), (), s32[]{:S(2)}) async-start(), calls=%async_computation.12 | async-start | bytes 8478720 | tf_op jit(solution)/shard_map/reduce_scatter | solution.py:253
  234.8 164.9 %collective-permute-start.1 = (bf16[1,729,1152]{2,1,0:T(8,128)(2,1)}, bf16[1,729,1152]{2,1,0:T(8,128)(2,1)}, u32[]{:S(2)}, u32[]{:S(2)}) collective-permute-start(bf16[1,729,1152]{2,1,0:T(8,128)(2,1)} %collective-permute-done), channel_id=1, source_target_pairs={{0,3},{1,0},{2,1},{3,2},{4,7},{5,4},{6,5},{7,6},{8,11},{9,8},{10,9... | collective-permute-start | bytes 5038856 | tf_op jit(solution)/shard_map/ppermute | solution.py:16
  384.9 19.4 %copy-start.10 = (bf16[4,729,1152]{2,1,0:T(8,128)(2,1)S(1)}, bf16[4,729,1152]{2,1,0:T(8,128)(2,1)}, u32[]{:S(2)}) copy-start(bf16[4,729,1152]{2,1,0:T(8,128)(2,1)} %all-gather.20.cloned.1.call-done) | copy-start | bytes 20155396
  399.7 62.0 %collective-permute-start.2 = (bf16[1,729,1152]{2,1,0:T(8,128)(2,1)}, bf16[1,729,1152]{2,1,0:T(8,128)(2,1)S(1)}, u32[]{:S(2)}, u32[]{:S(2)}) collective-permute-start(bf16[1,729,1152]{2,1,0:T(8,128)(2,1)} %collective-permute-done.1), channel_id=1, source_target_pairs={{0,3},{1,0},{2,1},{3,2},{4,7},{5,4},{6,5},{7,6},{8,11},{9,8},{10,9... | collective-permute-start | bytes 5038856 | tf_op jit(solution)/shard_map/ppermute | solution.py:16
  538.8 241.6 %reduce-scatter.7.cloned.1.call-start = ((), (), s32[]{:S(2)}) async-start(), calls=%async_computation.10 | async-start | bytes 8478720 | tf_op jit(solution)/shard_map/reduce_scatter | solution.py:228
  564.3 249.0 %all-gather.22.cloned.1.call-start = ((), (), s32[]{:S(2)}) async-start(), calls=%async_computation.13 | async-start | bytes 5087232 | tf_op jit(solution)/shard_map/all_gather | solution.py:272
  658.7 121.7 %copy-start.18 = (bf16[1,729,1152]{2,1,0:T(8,128)(2,1)S(1)}, bf16[1,729,1152]{2,1,0:T(8,128)(2,1)}, u32[]{:S(2)}) copy-start(bf16[1,729,1152]{2,1,0:T(8,128)(2,1)} %reduce-scatter.9.cloned.1.call-done) | copy-start | bytes 5038852
  786.8 175.6 %all-reduce.11.cloned.1.call-start = ((), (), s32[]{:S(2)}) async-start(), calls=%async_computation.17 | async-start | bytes 1179648 | tf_op jit(solution)/shard_map/psum | solution.py:336
  795.7 13.3 %slice-start = ((s8[6782976]{0:T(1024)(128)(4,1)}), s8[2588672]{0:T(1024)(128)(4,1)S(1)}, s32[]{:S(2)}) async-start(s8[6782976]{0:T(1024)(128)(4,1)} %bitcast.257), calls=%async_computation.18 | async-start | bytes 5177344
  813.2 236.5 %all-reduce.9.cloned.1.call-start = ((), (), s32[]{:S(2)}) async-start(), calls=%async_computation.16 | async-start | bytes 2621440 | tf_op jit(solution)/shard_map/psum | solution.py:332
  825.4 99.8 %copy-start.26 = (f32[3,2,729,16]{2,3,0,1:T(8,128)S(1)}, f32[3,2,729,16]{2,3,0,1:T(8,128)}, u32[]{:S(2)}) copy-start(f32[3,2,729,16]{2,3,0,1:T(8,128)} %copy-done.25) | copy-start | bytes 839812
  844.1 12.7 %copy-start.55 = (bf16[2,729,8,72]{1,3,2,0:T(8,128)(2,1)}, bf16[2,729,8,72]{1,3,2,0:T(8,128)(2,1)S(1)}, u32[]{:S(2)}) copy-start(bf16[2,729,8,72]{1,3,2,0:T(8,128)(2,1)S(1)} %bitcast_dynamic-update-slice_fusion.11) | copy-start | bytes 5038852 | tf_op jit(solution)/shard_map/while
  856.8 13.3 %copy-start.6 = (bf16[2,729,8,72]{1,3,2,0:T(8,128)(2,1)S(1)}, bf16[2,729,8,72]{1,3,2,0:T(8,128)(2,1)}, u32[]{:S(2)}) copy-start(bf16[2,729,8,72]{1,3,2,0:T(8,128)(2,1)} %get-tuple-element.355) | copy-start | bytes 5038852 | tf_op jit(solution)/shard_map/while
  856.8 13.3 %copy-start.57 = (bf16[2,729,8,72]{1,3,2,0:T(8,128)(2,1)S(1)}, bf16[2,729,8,72]{1,3,2,0:T(8,128)(2,1)}, u32[]{:S(2)}) copy-start(bf16[2,729,8,72]{1,3,2,0:T(8,128)(2,1)} %get-tuple-element.342) | copy-start | bytes 5038852 | tf_op jit(solution)/shard_map/while
  893.9 12.6 %copy-start.55 = (bf16[2,729,8,72]{1,3,2,0:T(8,128)(2,1)}, bf16[2,729,8,72]{1,3,2,0:T(8,128)(2,1)S(1)}, u32[]{:S(2)}) copy-start(bf16[2,729,8,72]{1,3,2,0:T(8,128)(2,1)S(1)} %bitcast_dynamic-update-slice_fusion.11) | copy-start | bytes 5038852 | tf_op jit(solution)/shard_map/while
  906.5 13.1 %copy-start.6 = (bf16[2,729,8,72]{1,3,2,0:T(8,128)(2,1)S(1)}, bf16[2,729,8,72]{1,3,2,0:T(8,128)(2,1)}, u32[]{:S(2)}) copy-start(bf16[2,729,8,72]{1,3,2,0:T(8,128)(2,1)} %get-tuple-element.355) | copy-start | bytes 5038852 | tf_op jit(solution)/shard_map/while
  906.5 13.1 %copy-start.57 = (bf16[2,729,8,72]{1,3,2,0:T(8,128)(2,1)S(1)}, bf16[2,729,8,72]{1,3,2,0:T(8,128)(2,1)}, u32[]{:S(2)}) copy-start(bf16[2,729,8,72]{1,3,2,0:T(8,128)(2,1)} %get-tuple-element.342) | copy-start | bytes 5038852 | tf_op jit(solution)/shard_map/while
  934.3 262.2 %all-reduce.7.cloned.1.call-start = ((), (), s32[]{:S(2)}) async-start(), calls=%async_computation.15 | async-start | bytes 7077888 | tf_op jit(solution)/shard_map/psum | solution.py:328
  945.6 263.5 %reduce-scatter.11.cloned.1.call-start = ((), (), s32[]{:S(2)}) async-start(), calls=%async_computation.14 | async-start | bytes 5087232 | tf_op jit(solution)/shard_map/reduce_scatter | solution.py:303
  (59 other events, 331.9 us)
Sparse Core Ops, SparseCore 0:
  17.1 15.1 all-gather.9
  34.2 55.7 all-gather.11
  91.9 30.1 all-gather.13
  177.6 11.2 reduce-scatter.4
  190.6 41.0 all-gather.17
  233.2 151.7 all-gather.19
  386.8 41.8 all-gather.15
  538.9 119.7 reduce-scatter.8
  661.1 119.1 reduce-scatter.6
  786.9 13.0 all-gather.21
  813.3 55.7 all-reduce.10
  934.5 115.1 all-reduce.8
  1056.8 139.7 all-reduce.6
  1198.8 10.2 reduce-scatter.10
